TPU v7x, 32 devices: a whole 2x2x4 slice. The times are simulated.
32 devices in a mesh: blade: 1, prow: 4 (over x, core), pcol: 8 (over z, y).
Axes of the slice: x: 2, y: 2, z: 4, core: 2. Of those that a mesh axis runs over, the one named last changes fastest.
Arguments:
- factor: float32 [4, 4, 512, 4, 8, 256], P('blade', 'prow', None, None, 'pcol'), may hold values from -0.03125 to 0.03125
- inverses: float32 [4, 8, 256, 4, 512], P('blade', 'pcol', None, 'prow'), as said below
- targets: float32 [8, 3, 8192], P('blade'), may hold values from -6 to 6
- anchors: float32 [3, 8192], P('blade'), may hold values from 0 to 1, as said below
- nodes: float32 [3, 16, 128, 128], P('blade', 'prow', 'pcol'), as said below
Outputs:
- coefficients: float32 [8, 3, 8192], P('blade')
- moved: float32 [8, 3, 16, 128, 128], P('blade', None, 'prow', 'pcol')
- jacobian: float32 [8, 16, 128, 128], P('blade', 'prow', 'pcol')
Inputs may be any that keep to these rules, and one draw needn't show every extreme that they name: `inverses`: 4 blocks of 2048 x 2048 real entries. `anchors`: positions in the unit cube. `nodes`: positions inside a box around the unit cube, ordered along span, chord and normal.
All inputs are finite; a program needn't handle non-finite values.
Results may differ from a plain program's by a relative error of at most 0.0003.
Values sent between devices are 32-bit elements; how exact they have to be, the bound alone decides.
A program may use at most 64 MiB of HBM per device.

v0:
```python
import math
import jax
import jax.numpy as jnp
from jax import lax
from jax.sharding import PartitionSpec as P

support_radius = 0.1
highest = lax.Precision.HIGHEST


def padded_2(cells, sides, width):
    for axis, dim in sides:
        count = lax.axis_size(axis)
        ends = count - 1
        head = lax.slice_in_dim(cells, 0, width, axis=dim)
        tail = lax.slice_in_dim(cells, cells.shape[dim] - width, cells.shape[dim], axis=dim)
        cells = jnp.concatenate(
            [
                lax.ppermute(tail, axis, [(i, (i + 1) % count) for i in range(ends)]),
                cells,
                lax.ppermute(head, axis, [((i + 1) % count, i) for i in range(ends)]),
            ],
            axis=dim,
        )
    return cells


def wendland(dist_sq):
    scaled_dist = jnp.sqrt(dist_sq) / support_radius
    falloff = jnp.maximum(1.0 - scaled_dist, 0.0)
    return falloff**4 * (4.0 * scaled_dist + 1.0)


def extend(values, axis_pos):
    extent = values.shape[axis_pos]
    low_layer = 2.0 * lax.slice_in_dim(values, 0, 1, axis=axis_pos) - lax.slice_in_dim(
        values, 1, 2, axis=axis_pos
    )
    high_layer = 2.0 * lax.slice_in_dim(
        values, extent - 1, extent, axis=axis_pos
    ) - lax.slice_in_dim(values, extent - 2, extent - 1, axis=axis_pos)
    return jnp.concatenate([low_layer, values, high_layer], axis=axis_pos)


def close_edges(padded, axis_pos, at_low, at_high):
    extent = padded.shape[axis_pos]
    low_layer = 2.0 * lax.slice_in_dim(padded, 1, 2, axis=axis_pos) - lax.slice_in_dim(
        padded, 2, 3, axis=axis_pos
    )
    high_layer = 2.0 * lax.slice_in_dim(
        padded, extent - 2, extent - 1, axis=axis_pos
    ) - lax.slice_in_dim(padded, extent - 3, extent - 2, axis=axis_pos)
    first_layer = jnp.where(at_low, low_layer, lax.slice_in_dim(padded, 0, 1, axis=axis_pos))
    last_layer = jnp.where(
        at_high, high_layer, lax.slice_in_dim(padded, extent - 1, extent, axis=axis_pos)
    )
    inner_layers = lax.slice_in_dim(padded, 1, extent - 1, axis=axis_pos)
    return jnp.concatenate([first_layer, inner_layers, last_layer], axis=axis_pos)


def jacobian_of(extended, scales):
    d_span = (extended[:, :, 2:, 1:-1, 1:-1] - extended[:, :, :-2, 1:-1, 1:-1]) * scales[0]
    d_chord = (extended[:, :, 1:-1, 2:, 1:-1] - extended[:, :, 1:-1, :-2, 1:-1]) * scales[1]
    d_normal = (extended[:, :, 1:-1, 1:-1, 2:] - extended[:, :, 1:-1, 1:-1, :-2]) * scales[2]
    cross_first = d_chord[:, 1] * d_normal[:, 2] - d_chord[:, 2] * d_normal[:, 1]
    cross_second = d_chord[:, 2] * d_normal[:, 0] - d_chord[:, 0] * d_normal[:, 2]
    cross_third = d_chord[:, 0] * d_normal[:, 1] - d_chord[:, 1] * d_normal[:, 0]
    return d_span[:, 0] * cross_first + d_span[:, 1] * cross_second + d_span[:, 2] * cross_third


def shards(factor, inverses, targets, anchors, nodes):
    row_devs = lax.axis_size("prow")
    col_devs = lax.axis_size("pcol")
    prow_id = lax.axis_index("prow")
    pcol_id = lax.axis_index("pcol")
    local_factor = factor[:, 0, :, :, 0, :]
    local_inverses = inverses[:, 0, :, 0, :]
    block_total = local_factor.shape[0]
    row_piece = local_factor.shape[1]
    col_piece = local_factor.shape[3]
    block_len = row_piece * row_devs
    instances = targets.shape[0]
    row_count = instances * targets.shape[1]
    point_total = targets.shape[2]
    right_sides = targets.reshape(row_count, block_total, block_len)
    forward = jnp.zeros((row_count, block_total, col_piece), jnp.float32)
    for block_id in range(block_total):
        partial_value = jnp.einsum(
            "rjc,wjc->wr", local_factor[block_id], forward, precision=highest
        )
        own_rows = lax.dynamic_slice_in_dim(
            right_sides[:, block_id], prow_id * row_piece, row_piece, 1
        )
        summed = lax.psum(partial_value, "pcol")
        term = jnp.einsum(
            "ab,wb->wa", local_inverses[block_id], own_rows - summed, precision=highest
        )
        solved = lax.psum(term, "prow")
        forward = forward.at[:, block_id].set(solved)
    coeffs = jnp.zeros((row_count, block_total, row_piece), jnp.float32)
    for block_id in reversed(range(block_total)):
        col_blocks = local_factor[:, :, block_id]
        forward_block = forward[:, block_id]
        partial_value = jnp.einsum("jrc,wjr->wc", col_blocks, coeffs, precision=highest)
        summed = lax.psum(partial_value, "prow")
        term = jnp.einsum(
            "ab,wa->wb", local_inverses[block_id], forward_block - summed, precision=highest
        )
        solved = lax.psum(term, "pcol")
        coeffs = coeffs.at[:, block_id].set(solved)
    coeffs = lax.all_gather(coeffs, "prow", axis=2, tiled=True)
    coef_matrix = coeffs.reshape(row_count, point_total)
    flat = nodes.reshape(3, -1)
    node_count = flat.shape[1]
    block_size = min(512, node_count)
    node_groups = flat.reshape(3, node_count // block_size, block_size).transpose(1, 0, 2)

    def deform(node_group):
        dist_sq = (node_group[0][:, None] - anchors[0][None, :]) ** 2
        dist_sq = dist_sq + (node_group[1][:, None] - anchors[1][None, :]) ** 2
        dist_sq = dist_sq + (node_group[2][:, None] - anchors[2][None, :]) ** 2
        return lax.dot_general(
            coef_matrix, wendland(dist_sq), (((1,), (1,)), ((), ())), precision=highest
        )

    shifts = lax.map(deform, node_groups)
    shifts = shifts.transpose(1, 0, 2).reshape((instances,) + nodes.shape)
    moved = nodes[None] + 2.0 / math.sqrt(point_total) * shifts
    padded = padded_2(moved, (("prow", 2), ("pcol", 3)), 1)
    padded = close_edges(padded, 2, prow_id == 0, prow_id == row_devs - 1)
    padded = close_edges(padded, 3, pcol_id == 0, pcol_id == col_devs - 1)
    extended = extend(padded, 4)
    scales = (
        nodes.shape[1] * row_devs / 2.0,
        nodes.shape[2] * col_devs / 2.0,
        nodes.shape[3] / 2.0,
    )
    jacobian = jacobian_of(extended, scales)
    return (coeffs.reshape(instances, 3, point_total), moved, jacobian)


def solution(mesh):
    placed = (
        P("blade", "prow", None, None, "pcol", None),
        P("blade", "pcol", None, "prow", None),
        P("blade", None, None),
        P("blade", None),
        P("blade", "prow", "pcol", None),
    )
    return jax.shard_map(
        shards,
        mesh=mesh,
        in_specs=placed,
        out_specs=(
            P("blade", None, None),
            P("blade", None, "prow", "pcol", None),
            P("blade", "prow", "pcol", None),
        ),
        check_vma=False,
    )
```

profile of v0, /device:TPU:1, one launch (start us, length us, event | category | flops | bytes accessed | tf_op | source)
XLA Modules:
  0.0 1282.0 jit_solution(8106645865025207151)
XLA Ops:
  31.5 32.1 %psum.112 = f32[24,512]{1,0:T(8,128)S(1)} all-reduce(f32[24,512]{1,0:T(8,128)} %fusion.58), channel_id=1, replica_groups=mesh['blade'=1,'prow'=4,'pcol'=8] {'pcol'}, use_global_device_ids=true, to_apply=%region_0.0 | all-reduce | flops 12288 | bytes 98304 | tf_op jit(solution)/shard_map/psum | solution.py:94
  90.3 27.0 %psum.114 = f32[24,512]{1,0:T(8,128)S(1)} all-reduce(f32[24,512]{1,0:T(8,128)} %fusion.61), channel_id=1, replica_groups=mesh['blade'=1,'prow'=4,'pcol'=8] {'pcol'}, use_global_device_ids=true, to_apply=%region_2.0 | all-reduce | flops 12288 | bytes 98304 | tf_op jit(solution)/shard_map/psum | solution.py:94
  141.6 28.3 %psum.116 = f32[24,512]{1,0:T(8,128)S(1)} all-reduce(f32[24,512]{1,0:T(8,128)S(1)} %fusion.64), channel_id=1, replica_groups=mesh['blade'=1,'prow'=4,'pcol'=8] {'pcol'}, use_global_device_ids=true, to_apply=%region_4.0 | all-reduce | flops 12288 | bytes 98304 | tf_op jit(solution)/shard_map/psum | solution.py:94
  196.0 27.0 %psum.118 = f32[24,512]{1,0:T(8,128)S(1)} all-reduce(f32[24,512]{1,0:T(8,128)} %fusion.67), channel_id=1, replica_groups=mesh['blade'=1,'prow'=4,'pcol'=8] {'pcol'}, use_global_device_ids=true, to_apply=%region_6.0 | all-reduce | flops 12288 | bytes 98304 | tf_op jit(solution)/shard_map/psum | solution.py:94
  263.5 28.2 %psum.121 = f32[24,1,512]{2,0,1:T(8,128)S(1)} all-reduce(f32[24,1,512]{2,0,1:T(8,128)S(1)} %convolution_bitcast_fusion.3), channel_id=1, replica_groups=mesh['blade'=1,'prow'=4,'pcol'=8] {'pcol'}, use_global_device_ids=true, to_apply=%region_9.0 | all-reduce | flops 12288 | bytes 98304 | tf_op jit(solution)/shard_map/psum | solution.py:109
  313.8 26.5 %psum.123 = f32[24,1,512]{2,0,1:T(8,128)S(1)} all-reduce(f32[24,1,512]{2,0,1:T(8,128)S(1)} %convolution_bitcast_fusion.2), channel_id=1, replica_groups=mesh['blade'=1,'prow'=4,'pcol'=8] {'pcol'}, use_global_device_ids=true, to_apply=%region_11.0 | all-reduce | flops 12288 | bytes 98304 | tf_op jit(solution)/shard_map/psum | solution.py:109
  360.4 28.2 %psum.125 = f32[24,1,512]{2,0,1:T(8,128)S(1)} all-reduce(f32[24,1,512]{2,0,1:T(8,128)S(1)} %convolution_bitcast_fusion.1), channel_id=1, replica_groups=mesh['blade'=1,'prow'=4,'pcol'=8] {'pcol'}, use_global_device_ids=true, to_apply=%region_13.0 | all-reduce | flops 12288 | bytes 98304 | tf_op jit(solution)/shard_map/psum | solution.py:109
  450.1 808.1 %while.20 = (s32[]{:T(128)}, f32[16,24,512]{2,1,0:T(8,128)S(1)}, f32[16,3,512]{2,0,1:T(8,128)S(1)}, f32[3,8192]{1,0:T(4,128)S(1)}, f32[24,8192]{1,0:T(8,128)S(1)}, /*index=5*/s32[]{:T(128)}, s32[]{:T(128)}, s32[]{}, s32[]{}) while((s32[]{:T(128)}, f32[16,24,512]{2,1,0:T(8,128)S(1)}, f32[16,3,512]{2,0,1:T(8,128)S(1)}, ...), condition=%wide.region_17.0_spmd, body=%wide.region_16.0_spmd.sunk | while | flops 1275068416 | bytes 1149061 | solution.py:126
  450.2 50.4 %fusion.144 = f32[16,24,512]{2,1,0:T(8,128)S(1)} fusion(f32[16,24,512]{2,1,0:T(8,128)S(1)} %get-tuple-element.271, s32[]{:T(128)} %get-tuple-element.270, f32[24,8192]{1,0:T(8,128)S(1)} %get-tuple-element.283, f32[8192]{0:T(1024)S(1)} %bitcast.168, f32[512]{0:T(512)S(1)} %bitcast.174, f32[8192]{0:T(1024)S(1)} %bitcast.169, f32[512]{0:T(512)S(1)} %bitcast.173, ...), kind=kOutput, calls=%fused_computation.29.clone.1 | convolution fusion | flops 1275068416 | bytes 940036 | tf_op jit(solution)/shard_map/while/body/eval_jaxpr/dot_general | solution.py:122
  500.7 50.4 %fusion.144 = f32[16,24,512]{2,1,0:T(8,128)S(1)} fusion(f32[16,24,512]{2,1,0:T(8,128)S(1)} %get-tuple-element.271, s32[]{:T(128)} %get-tuple-element.270, f32[24,8192]{1,0:T(8,128)S(1)} %get-tuple-element.283, f32[8192]{0:T(1024)S(1)} %bitcast.168, f32[512]{0:T(512)S(1)} %bitcast.174, f32[8192]{0:T(1024)S(1)} %bitcast.169, f32[512]{0:T(512)S(1)} %bitcast.173, ...), kind=kOutput, calls=%fused_computation.29.clone.1 | convolution fusion | flops 1275068416 | bytes 940036 | tf_op jit(solution)/shard_map/while/body/eval_jaxpr/dot_general | solution.py:122
  551.2 50.4 %fusion.144 = f32[16,24,512]{2,1,0:T(8,128)S(1)} fusion(f32[16,24,512]{2,1,0:T(8,128)S(1)} %get-tuple-element.271, s32[]{:T(128)} %get-tuple-element.270, f32[24,8192]{1,0:T(8,128)S(1)} %get-tuple-element.283, f32[8192]{0:T(1024)S(1)} %bitcast.168, f32[512]{0:T(512)S(1)} %bitcast.174, f32[8192]{0:T(1024)S(1)} %bitcast.169, f32[512]{0:T(512)S(1)} %bitcast.173, ...), kind=kOutput, calls=%fused_computation.29.clone.1 | convolution fusion | flops 1275068416 | bytes 940036 | tf_op jit(solution)/shard_map/while/body/eval_jaxpr/dot_general | solution.py:122
  601.7 50.4 %fusion.144 = f32[16,24,512]{2,1,0:T(8,128)S(1)} fusion(f32[16,24,512]{2,1,0:T(8,128)S(1)} %get-tuple-element.271, s32[]{:T(128)} %get-tuple-element.270, f32[24,8192]{1,0:T(8,128)S(1)} %get-tuple-element.283, f32[8192]{0:T(1024)S(1)} %bitcast.168, f32[512]{0:T(512)S(1)} %bitcast.174, f32[8192]{0:T(1024)S(1)} %bitcast.169, f32[512]{0:T(512)S(1)} %bitcast.173, ...), kind=kOutput, calls=%fused_computation.29.clone.1 | convolution fusion | flops 1275068416 | bytes 940036 | tf_op jit(solution)/shard_map/while/body/eval_jaxpr/dot_general | solution.py:122
  652.2 50.4 %fusion.144 = f32[16,24,512]{2,1,0:T(8,128)S(1)} fusion(f32[16,24,512]{2,1,0:T(8,128)S(1)} %get-tuple-element.271, s32[]{:T(128)} %get-tuple-element.270, f32[24,8192]{1,0:T(8,128)S(1)} %get-tuple-element.283, f32[8192]{0:T(1024)S(1)} %bitcast.168, f32[512]{0:T(512)S(1)} %bitcast.174, f32[8192]{0:T(1024)S(1)} %bitcast.169, f32[512]{0:T(512)S(1)} %bitcast.173, ...), kind=kOutput, calls=%fused_computation.29.clone.1 | convolution fusion | flops 1275068416 | bytes 940036 | tf_op jit(solution)/shard_map/while/body/eval_jaxpr/dot_general | solution.py:122
  702.7 50.4 %fusion.144 = f32[16,24,512]{2,1,0:T(8,128)S(1)} fusion(f32[16,24,512]{2,1,0:T(8,128)S(1)} %get-tuple-element.271, s32[]{:T(128)} %get-tuple-element.270, f32[24,8192]{1,0:T(8,128)S(1)} %get-tuple-element.283, f32[8192]{0:T(1024)S(1)} %bitcast.168, f32[512]{0:T(512)S(1)} %bitcast.174, f32[8192]{0:T(1024)S(1)} %bitcast.169, f32[512]{0:T(512)S(1)} %bitcast.173, ...), kind=kOutput, calls=%fused_computation.29.clone.1 | convolution fusion | flops 1275068416 | bytes 940036 | tf_op jit(solution)/shard_map/while/body/eval_jaxpr/dot_general | solution.py:122
  753.3 50.4 %fusion.144 = f32[16,24,512]{2,1,0:T(8,128)S(1)} fusion(f32[16,24,512]{2,1,0:T(8,128)S(1)} %get-tuple-element.271, s32[]{:T(128)} %get-tuple-element.270, f32[24,8192]{1,0:T(8,128)S(1)} %get-tuple-element.283, f32[8192]{0:T(1024)S(1)} %bitcast.168, f32[512]{0:T(512)S(1)} %bitcast.174, f32[8192]{0:T(1024)S(1)} %bitcast.169, f32[512]{0:T(512)S(1)} %bitcast.173, ...), kind=kOutput, calls=%fused_computation.29.clone.1 | convolution fusion | flops 1275068416 | bytes 940036 | tf_op jit(solution)/shard_map/while/body/eval_jaxpr/dot_general | solution.py:122
  803.8 50.4 %fusion.144 = f32[16,24,512]{2,1,0:T(8,128)S(1)} fusion(f32[16,24,512]{2,1,0:T(8,128)S(1)} %get-tuple-element.271, s32[]{:T(128)} %get-tuple-element.270, f32[24,8192]{1,0:T(8,128)S(1)} %get-tuple-element.283, f32[8192]{0:T(1024)S(1)} %bitcast.168, f32[512]{0:T(512)S(1)} %bitcast.174, f32[8192]{0:T(1024)S(1)} %bitcast.169, f32[512]{0:T(512)S(1)} %bitcast.173, ...), kind=kOutput, calls=%fused_computation.29.clone.1 | convolution fusion | flops 1275068416 | bytes 940036 | tf_op jit(solution)/shard_map/while/body/eval_jaxpr/dot_general | solution.py:122
  854.3 50.4 %fusion.144 = f32[16,24,512]{2,1,0:T(8,128)S(1)} fusion(f32[16,24,512]{2,1,0:T(8,128)S(1)} %get-tuple-element.271, s32[]{:T(128)} %get-tuple-element.270, f32[24,8192]{1,0:T(8,128)S(1)} %get-tuple-element.283, f32[8192]{0:T(1024)S(1)} %bitcast.168, f32[512]{0:T(512)S(1)} %bitcast.174, f32[8192]{0:T(1024)S(1)} %bitcast.169, f32[512]{0:T(512)S(1)} %bitcast.173, ...), kind=kOutput, calls=%fused_computation.29.clone.1 | convolution fusion | flops 1275068416 | bytes 940036 | tf_op jit(solution)/shard_map/while/body/eval_jaxpr/dot_general | solution.py:122
  904.8 50.4 %fusion.144 = f32[16,24,512]{2,1,0:T(8,128)S(1)} fusion(f32[16,24,512]{2,1,0:T(8,128)S(1)} %get-tuple-element.271, s32[]{:T(128)} %get-tuple-element.270, f32[24,8192]{1,0:T(8,128)S(1)} %get-tuple-element.283, f32[8192]{0:T(1024)S(1)} %bitcast.168, f32[512]{0:T(512)S(1)} %bitcast.174, f32[8192]{0:T(1024)S(1)} %bitcast.169, f32[512]{0:T(512)S(1)} %bitcast.173, ...), kind=kOutput, calls=%fused_computation.29.clone.1 | convolution fusion | flops 1275068416 | bytes 940036 | tf_op jit(solution)/shard_map/while/body/eval_jaxpr/dot_general | solution.py:122
  955.3 50.4 %fusion.144 = f32[16,24,512]{2,1,0:T(8,128)S(1)} fusion(f32[16,24,512]{2,1,0:T(8,128)S(1)} %get-tuple-element.271, s32[]{:T(128)} %get-tuple-element.270, f32[24,8192]{1,0:T(8,128)S(1)} %get-tuple-element.283, f32[8192]{0:T(1024)S(1)} %bitcast.168, f32[512]{0:T(512)S(1)} %bitcast.174, f32[8192]{0:T(1024)S(1)} %bitcast.169, f32[512]{0:T(512)S(1)} %bitcast.173, ...), kind=kOutput, calls=%fused_computation.29.clone.1 | convolution fusion | flops 1275068416 | bytes 940036 | tf_op jit(solution)/shard_map/while/body/eval_jaxpr/dot_general | solution.py:122
  1005.8 50.4 %fusion.144 = f32[16,24,512]{2,1,0:T(8,128)S(1)} fusion(f32[16,24,512]{2,1,0:T(8,128)S(1)} %get-tuple-element.271, s32[]{:T(128)} %get-tuple-element.270, f32[24,8192]{1,0:T(8,128)S(1)} %get-tuple-element.283, f32[8192]{0:T(1024)S(1)} %bitcast.168, f32[512]{0:T(512)S(1)} %bitcast.174, f32[8192]{0:T(1024)S(1)} %bitcast.169, f32[512]{0:T(512)S(1)} %bitcast.173, ...), kind=kOutput, calls=%fused_computation.29.clone.1 | convolution fusion | flops 1275068416 | bytes 940036 | tf_op jit(solution)/shard_map/while/body/eval_jaxpr/dot_general | solution.py:122
  1056.3 50.4 %fusion.144 = f32[16,24,512]{2,1,0:T(8,128)S(1)} fusion(f32[16,24,512]{2,1,0:T(8,128)S(1)} %get-tuple-element.271, s32[]{:T(128)} %get-tuple-element.270, f32[24,8192]{1,0:T(8,128)S(1)} %get-tuple-element.283, f32[8192]{0:T(1024)S(1)} %bitcast.168, f32[512]{0:T(512)S(1)} %bitcast.174, f32[8192]{0:T(1024)S(1)} %bitcast.169, f32[512]{0:T(512)S(1)} %bitcast.173, ...), kind=kOutput, calls=%fused_computation.29.clone.1 | convolution fusion | flops 1275068416 | bytes 940036 | tf_op jit(solution)/shard_map/while/body/eval_jaxpr/dot_general | solution.py:122
  1106.8 50.4 %fusion.144 = f32[16,24,512]{2,1,0:T(8,128)S(1)} fusion(f32[16,24,512]{2,1,0:T(8,128)S(1)} %get-tuple-element.271, s32[]{:T(128)} %get-tuple-element.270, f32[24,8192]{1,0:T(8,128)S(1)} %get-tuple-element.283, f32[8192]{0:T(1024)S(1)} %bitcast.168, f32[512]{0:T(512)S(1)} %bitcast.174, f32[8192]{0:T(1024)S(1)} %bitcast.169, f32[512]{0:T(512)S(1)} %bitcast.173, ...), kind=kOutput, calls=%fused_computation.29.clone.1 | convolution fusion | flops 1275068416 | bytes 940036 | tf_op jit(solution)/shard_map/while/body/eval_jaxpr/dot_general | solution.py:122
  1157.3 50.4 %fusion.144 = f32[16,24,512]{2,1,0:T(8,128)S(1)} fusion(f32[16,24,512]{2,1,0:T(8,128)S(1)} %get-tuple-element.271, s32[]{:T(128)} %get-tuple-element.270, f32[24,8192]{1,0:T(8,128)S(1)} %get-tuple-element.283, f32[8192]{0:T(1024)S(1)} %bitcast.168, f32[512]{0:T(512)S(1)} %bitcast.174, f32[8192]{0:T(1024)S(1)} %bitcast.169, f32[512]{0:T(512)S(1)} %bitcast.173, ...), kind=kOutput, calls=%fused_computation.29.clone.1 | convolution fusion | flops 1275068416 | bytes 940036 | tf_op jit(solution)/shard_map/while/body/eval_jaxpr/dot_general | solution.py:122
  1207.8 50.4 %fusion.144 = f32[16,24,512]{2,1,0:T(8,128)S(1)} fusion(f32[16,24,512]{2,1,0:T(8,128)S(1)} %get-tuple-element.271, s32[]{:T(128)} %get-tuple-element.270, f32[24,8192]{1,0:T(8,128)S(1)} %get-tuple-element.283, f32[8192]{0:T(1024)S(1)} %bitcast.168, f32[512]{0:T(512)S(1)} %bitcast.174, f32[8192]{0:T(1024)S(1)} %bitcast.169, f32[512]{0:T(512)S(1)} %bitcast.173, ...), kind=kOutput, calls=%fused_computation.29.clone.1 | convolution fusion | flops 1275068416 | bytes 940036 | tf_op jit(solution)/shard_map/while/body/eval_jaxpr/dot_general | solution.py:122
  (129 shorter events, 276.9 us)
Async XLA Ops:
  9.9 8.8 copy-start.5
  243.1 1.0 copy-start
  389.5 60.5 %copy-start.3 = (f32[3,4,16,128]{3,2,1,0:T(8,128)S(1)}, f32[3,4,16,128]{3,2,1,0:T(8,128)}, u32[]{:S(2)}) copy-start(f32[3,4,16,128]{3,2,1,0:T(8,128)} %param.27) | copy-start | bytes 294916
  389.5 60.5 %copy-start.1 = (f32[3,8192]{1,0:T(4,128)S(1)}, f32[3,8192]{1,0:T(4,128)}, u32[]{:S(2)}) copy-start(f32[3,8192]{1,0:T(4,128)} %param.26) | copy-start | bytes 294916
  389.6 60.5 %copy-start.6 = (f32[16,24,512]{2,1,0:T(8,128)S(1)}, f32[16,24,512]{2,1,0:T(8,128)}, u32[]{:S(2)}) copy-start(f32[16,24,512]{2,1,0:T(8,128)} %custom-call.1) | copy-start | bytes 2359300
  1258.8 4.7 copy-start.4
  1258.9 9.8 copy-start.2
  1259.0 4.6 collective-permute-start
  1261.0 7.0 collective-permute-start.1
  1268.8 5.8 collective-permute-start.2
  1270.7 5.4 collective-permute-start.3
where the time goes:
time: 1280 us
  matrix products  827 us (65%)
  blocking collectives  363 us (28%)
  local copies, waits for them, and re-layouts  71.1 us (6%)
    dot_general x16, matrix products, deform(): lax.dot_general(coef_matrix, wendland(dist_sq), (((1,), (1,)), ((), ())),...  806 us
    psum x4, blocking collectives, shards(): summed = lax.psum(partial_value, 'pcol')  114 us
    psum x4, blocking collectives, shards(): solved = lax.psum(term, 'pcol')  109 us
    psum x4, blocking collectives, shards(): solved = lax.psum(term, 'prow')  70.5 us
    psum x3, blocking collectives, shards(): summed = lax.psum(partial_value, 'prow')  52.8 us
  transfers between devices with their start and end apart: 4, of which 3 were waited for; matrix products, arithmetic and copies ran while one was open for 0% of the time, Pallas kernels for 0%

commit v1 on v0

--- a/solution.py
+++ b/solution.py
@@ -102,7 +102,9 @@
         col_blocks = local_factor[:, :, block_id]
         forward_block = forward[:, block_id]
         partial_value = jnp.einsum("jrc,wjr->wc", col_blocks, coeffs, precision=highest)
-        summed = lax.psum(partial_value, "prow")
+        summed = partial_value
+        for hop in (1, 2):
+            summed = summed + lax.ppermute(summed, "prow", [(dev, dev ^ hop) for dev in range(4)])
         term = jnp.einsum(
             "ab,wa->wb", local_inverses[block_id], forward_block - summed, precision=highest
         )

time: 1280 us -> 1240 us (0.969)
  blocking collectives: 363 us -> 308 us
  starting transfers between devices: 7.53 us -> 37.3 us
  local copies, waits for them, and re-layouts: 71.1 us -> 43.9 us
    psum x3 -> x0, blocking collectives: 52.8 us -> none  [shards(): summed = lax.psum(partial_value, 'prow')]
    ppermute x0 -> x8, starting transfers between devices: none -> 26.2 us  [shards(): lax.ppermute(summed, 'prow', [(dev, dev ^ hop) for dev in range(4)])]
    slice x1 -> x0, local copies, waits for them, and re-layouts: 20.1 us -> none  [shards(): col_blocks = local_factor[:, :, block_id]]
  transfers between devices with their start and end apart: 4 -> 12, of which waited for: 3 -> 8; matrix products, arithmetic and copies ran while one was open for 0% -> 4% of each run, Pallas kernels for 0% -> 0%
where the time goes in v1:
time: 1240 us
  matrix products  826 us (67%)
  blocking collectives  308 us (25%)
  local copies, waits for them, and re-layouts  43.9 us (4%)
  starting transfers between devices  37.3 us (3%)
  waiting for transfers between devices  15.3 us (1%)
    dot_general x16, matrix products, deform(): lax.dot_general(coef_matrix, wendland(dist_sq), (((1,), (1,)), ((), ())),...  806 us
    psum x4, blocking collectives, shards(): summed = lax.psum(partial_value, 'pcol')  114 us
    psum x4, blocking collectives, shards(): solved = lax.psum(term, 'pcol')  110 us
    psum x4, blocking collectives, shards(): solved = lax.psum(term, 'prow')  68.8 us
    ppermute x8, starting transfers between devices, shards(): lax.ppermute(summed, 'prow', [(dev, dev ^ hop) for dev in range(4)])  26.2 us
  transfers between devices with their start and end apart: 12, of which 8 were waited for; matrix products, arithmetic and copies ran while one was open for 4% of the time, Pallas kernels for 0%

profile of v1, /device:TPU:1, one launch (start us, length us, event | category | flops | bytes accessed | tf_op | source)
XLA Modules:
  0.0 1239.0 jit_solution(10649028044424494560)
XLA Ops:
  21.9 32.4 %psum.84 = f32[24,512]{1,0:T(8,128)S(1)} all-reduce(f32[24,512]{1,0:T(8,128)S(1)} %fusion.50), channel_id=1, replica_groups=mesh['blade'=1,'prow'=4,'pcol'=8] {'pcol'}, use_global_device_ids=true, to_apply=%region_0.0 | all-reduce | flops 12288 | bytes 98304 | tf_op jit(solution)/shard_map/psum | solution.py:94
  81.1 26.6 %psum.86 = f32[24,512]{1,0:T(8,128)S(1)} all-reduce(f32[24,512]{1,0:T(8,128)S(1)} %fusion.53), channel_id=1, replica_groups=mesh['blade'=1,'prow'=4,'pcol'=8] {'pcol'}, use_global_device_ids=true, to_apply=%region_2.0 | all-reduce | flops 12288 | bytes 98304 | tf_op jit(solution)/shard_map/psum | solution.py:94
  132.0 28.2 %psum.88 = f32[24,512]{1,0:T(8,128)S(1)} all-reduce(f32[24,512]{1,0:T(8,128)S(1)} %fusion.56), channel_id=1, replica_groups=mesh['blade'=1,'prow'=4,'pcol'=8] {'pcol'}, use_global_device_ids=true, to_apply=%region_4.0 | all-reduce | flops 12288 | bytes 98304 | tf_op jit(solution)/shard_map/psum | solution.py:94
  185.5 26.6 %psum.90 = f32[24,512]{1,0:T(8,128)S(1)} all-reduce(f32[24,512]{1,0:T(8,128)S(1)} %fusion.59), channel_id=1, replica_groups=mesh['blade'=1,'prow'=4,'pcol'=8] {'pcol'}, use_global_device_ids=true, to_apply=%region_6.0 | all-reduce | flops 12288 | bytes 98304 | tf_op jit(solution)/shard_map/psum | solution.py:94
  234.4 28.1 %psum.92 = f32[24,1,512]{2,0,1:T(8,128)S(1)} all-reduce(f32[24,1,512]{2,0,1:T(8,128)S(1)} %convolution_bitcast_fusion.3), channel_id=1, replica_groups=mesh['blade'=1,'prow'=4,'pcol'=8] {'pcol'}, use_global_device_ids=true, to_apply=%region_8.0 | all-reduce | flops 12288 | bytes 98304 | tf_op jit(solution)/shard_map/psum | solution.py:111
  318.5 28.5 %psum.94 = f32[24,1,512]{2,0,1:T(8,128)S(1)} all-reduce(f32[24,1,512]{2,0,1:T(8,128)S(1)} %convolution_bitcast_fusion.1), channel_id=1, replica_groups=mesh['blade'=1,'prow'=4,'pcol'=8] {'pcol'}, use_global_device_ids=true, to_apply=%region_10.0 | all-reduce | flops 12288 | bytes 98304 | tf_op jit(solution)/shard_map/psum | solution.py:111
  361.8 26.7 %psum.95 = f32[24,1,512]{2,0,1:T(8,128)S(1)} all-reduce(f32[24,1,512]{2,0,1:T(8,128)S(1)} %convolution_bitcast_fusion), channel_id=1, replica_groups=mesh['blade'=1,'prow'=4,'pcol'=8] {'pcol'}, use_global_device_ids=true, to_apply=%region_11.0 | all-reduce | flops 12288 | bytes 98304 | tf_op jit(solution)/shard_map/psum | solution.py:111
  404.5 808.1 %while.20 = (s32[]{:T(128)}, f32[16,24,512]{2,1,0:T(8,128)S(1)}, f32[16,3,512]{2,0,1:T(8,128)S(1)}, f32[3,8192]{1,0:T(4,128)S(1)}, f32[24,8192]{1,0:T(8,128)S(1)}, /*index=5*/s32[]{:T(128)}, s32[]{:T(128)}, s32[]{}, s32[]{}) while((s32[]{:T(128)}, f32[16,24,512]{2,1,0:T(8,128)S(1)}, f32[16,3,512]{2,0,1:T(8,128)S(1)}, ...), condition=%wide.region_13.0_spmd, body=%wide.region_12.0_spmd.sunk | while | flops 1275068416 | bytes 1149069 | solution.py:128
  404.6 50.4 %fusion.131 = f32[16,24,512]{2,1,0:T(8,128)S(1)} fusion(f32[16,24,512]{2,1,0:T(8,128)S(1)} %get-tuple-element.265, s32[]{:T(128)S(6)} %copy.108, f32[24,8192]{1,0:T(8,128)S(1)} %get-tuple-element.277, f32[8192]{0:T(1024)S(1)} %bitcast.171, f32[512]{0:T(512)S(1)} %bitcast.177, f32[8192]{0:T(1024)S(1)} %bitcast.172, f32[512]{0:T(512)S(1)} %bitcast.176, ...), kind=kOutput, calls=%fused_computation.29.clone.1 | convolution fusion | flops 1275068416 | bytes 940036 | tf_op jit(solution)/shard_map/while/body/eval_jaxpr/dot_general | solution.py:124
  455.1 50.4 %fusion.131 = f32[16,24,512]{2,1,0:T(8,128)S(1)} fusion(f32[16,24,512]{2,1,0:T(8,128)S(1)} %get-tuple-element.265, s32[]{:T(128)S(6)} %copy.108, f32[24,8192]{1,0:T(8,128)S(1)} %get-tuple-element.277, f32[8192]{0:T(1024)S(1)} %bitcast.171, f32[512]{0:T(512)S(1)} %bitcast.177, f32[8192]{0:T(1024)S(1)} %bitcast.172, f32[512]{0:T(512)S(1)} %bitcast.176, ...), kind=kOutput, calls=%fused_computation.29.clone.1 | convolution fusion | flops 1275068416 | bytes 940036 | tf_op jit(solution)/shard_map/while/body/eval_jaxpr/dot_general | solution.py:124
  505.6 50.4 %fusion.131 = f32[16,24,512]{2,1,0:T(8,128)S(1)} fusion(f32[16,24,512]{2,1,0:T(8,128)S(1)} %get-tuple-element.265, s32[]{:T(128)S(6)} %copy.108, f32[24,8192]{1,0:T(8,128)S(1)} %get-tuple-element.277, f32[8192]{0:T(1024)S(1)} %bitcast.171, f32[512]{0:T(512)S(1)} %bitcast.177, f32[8192]{0:T(1024)S(1)} %bitcast.172, f32[512]{0:T(512)S(1)} %bitcast.176, ...), kind=kOutput, calls=%fused_computation.29.clone.1 | convolution fusion | flops 1275068416 | bytes 940036 | tf_op jit(solution)/shard_map/while/body/eval_jaxpr/dot_general | solution.py:124
  556.2 50.4 %fusion.131 = f32[16,24,512]{2,1,0:T(8,128)S(1)} fusion(f32[16,24,512]{2,1,0:T(8,128)S(1)} %get-tuple-element.265, s32[]{:T(128)S(6)} %copy.108, f32[24,8192]{1,0:T(8,128)S(1)} %get-tuple-element.277, f32[8192]{0:T(1024)S(1)} %bitcast.171, f32[512]{0:T(512)S(1)} %bitcast.177, f32[8192]{0:T(1024)S(1)} %bitcast.172, f32[512]{0:T(512)S(1)} %bitcast.176, ...), kind=kOutput, calls=%fused_computation.29.clone.1 | convolution fusion | flops 1275068416 | bytes 940036 | tf_op jit(solution)/shard_map/while/body/eval_jaxpr/dot_general | solution.py:124
  606.7 50.4 %fusion.131 = f32[16,24,512]{2,1,0:T(8,128)S(1)} fusion(f32[16,24,512]{2,1,0:T(8,128)S(1)} %get-tuple-element.265, s32[]{:T(128)S(6)} %copy.108, f32[24,8192]{1,0:T(8,128)S(1)} %get-tuple-element.277, f32[8192]{0:T(1024)S(1)} %bitcast.171, f32[512]{0:T(512)S(1)} %bitcast.177, f32[8192]{0:T(1024)S(1)} %bitcast.172, f32[512]{0:T(512)S(1)} %bitcast.176, ...), kind=kOutput, calls=%fused_computation.29.clone.1 | convolution fusion | flops 1275068416 | bytes 940036 | tf_op jit(solution)/shard_map/while/body/eval_jaxpr/dot_general | solution.py:124
  657.2 50.4 %fusion.131 = f32[16,24,512]{2,1,0:T(8,128)S(1)} fusion(f32[16,24,512]{2,1,0:T(8,128)S(1)} %get-tuple-element.265, s32[]{:T(128)S(6)} %copy.108, f32[24,8192]{1,0:T(8,128)S(1)} %get-tuple-element.277, f32[8192]{0:T(1024)S(1)} %bitcast.171, f32[512]{0:T(512)S(1)} %bitcast.177, f32[8192]{0:T(1024)S(1)} %bitcast.172, f32[512]{0:T(512)S(1)} %bitcast.176, ...), kind=kOutput, calls=%fused_computation.29.clone.1 | convolution fusion | flops 1275068416 | bytes 940036 | tf_op jit(solution)/shard_map/while/body/eval_jaxpr/dot_general | solution.py:124
  707.7 50.4 %fusion.131 = f32[16,24,512]{2,1,0:T(8,128)S(1)} fusion(f32[16,24,512]{2,1,0:T(8,128)S(1)} %get-tuple-element.265, s32[]{:T(128)S(6)} %copy.108, f32[24,8192]{1,0:T(8,128)S(1)} %get-tuple-element.277, f32[8192]{0:T(1024)S(1)} %bitcast.171, f32[512]{0:T(512)S(1)} %bitcast.177, f32[8192]{0:T(1024)S(1)} %bitcast.172, f32[512]{0:T(512)S(1)} %bitcast.176, ...), kind=kOutput, calls=%fused_computation.29.clone.1 | convolution fusion | flops 1275068416 | bytes 940036 | tf_op jit(solution)/shard_map/while/body/eval_jaxpr/dot_general | solution.py:124
  758.2 50.4 %fusion.131 = f32[16,24,512]{2,1,0:T(8,128)S(1)} fusion(f32[16,24,512]{2,1,0:T(8,128)S(1)} %get-tuple-element.265, s32[]{:T(128)S(6)} %copy.108, f32[24,8192]{1,0:T(8,128)S(1)} %get-tuple-element.277, f32[8192]{0:T(1024)S(1)} %bitcast.171, f32[512]{0:T(512)S(1)} %bitcast.177, f32[8192]{0:T(1024)S(1)} %bitcast.172, f32[512]{0:T(512)S(1)} %bitcast.176, ...), kind=kOutput, calls=%fused_computation.29.clone.1 | convolution fusion | flops 1275068416 | bytes 940036 | tf_op jit(solution)/shard_map/while/body/eval_jaxpr/dot_general | solution.py:124
  808.7 50.4 %fusion.131 = f32[16,24,512]{2,1,0:T(8,128)S(1)} fusion(f32[16,24,512]{2,1,0:T(8,128)S(1)} %get-tuple-element.265, s32[]{:T(128)S(6)} %copy.108, f32[24,8192]{1,0:T(8,128)S(1)} %get-tuple-element.277, f32[8192]{0:T(1024)S(1)} %bitcast.171, f32[512]{0:T(512)S(1)} %bitcast.177, f32[8192]{0:T(1024)S(1)} %bitcast.172, f32[512]{0:T(512)S(1)} %bitcast.176, ...), kind=kOutput, calls=%fused_computation.29.clone.1 | convolution fusion | flops 1275068416 | bytes 940036 | tf_op jit(solution)/shard_map/while/body/eval_jaxpr/dot_general | solution.py:124
  859.2 50.4 %fusion.131 = f32[16,24,512]{2,1,0:T(8,128)S(1)} fusion(f32[16,24,512]{2,1,0:T(8,128)S(1)} %get-tuple-element.265, s32[]{:T(128)S(6)} %copy.108, f32[24,8192]{1,0:T(8,128)S(1)} %get-tuple-element.277, f32[8192]{0:T(1024)S(1)} %bitcast.171, f32[512]{0:T(512)S(1)} %bitcast.177, f32[8192]{0:T(1024)S(1)} %bitcast.172, f32[512]{0:T(512)S(1)} %bitcast.176, ...), kind=kOutput, calls=%fused_computation.29.clone.1 | convolution fusion | flops 1275068416 | bytes 940036 | tf_op jit(solution)/shard_map/while/body/eval_jaxpr/dot_general | solution.py:124
  909.7 50.4 %fusion.131 = f32[16,24,512]{2,1,0:T(8,128)S(1)} fusion(f32[16,24,512]{2,1,0:T(8,128)S(1)} %get-tuple-element.265, s32[]{:T(128)S(6)} %copy.108, f32[24,8192]{1,0:T(8,128)S(1)} %get-tuple-element.277, f32[8192]{0:T(1024)S(1)} %bitcast.171, f32[512]{0:T(512)S(1)} %bitcast.177, f32[8192]{0:T(1024)S(1)} %bitcast.172, f32[512]{0:T(512)S(1)} %bitcast.176, ...), kind=kOutput, calls=%fused_computation.29.clone.1 | convolution fusion | flops 1275068416 | bytes 940036 | tf_op jit(solution)/shard_map/while/body/eval_jaxpr/dot_general | solution.py:124
  960.2 50.4 %fusion.131 = f32[16,24,512]{2,1,0:T(8,128)S(1)} fusion(f32[16,24,512]{2,1,0:T(8,128)S(1)} %get-tuple-element.265, s32[]{:T(128)S(6)} %copy.108, f32[24,8192]{1,0:T(8,128)S(1)} %get-tuple-element.277, f32[8192]{0:T(1024)S(1)} %bitcast.171, f32[512]{0:T(512)S(1)} %bitcast.177, f32[8192]{0:T(1024)S(1)} %bitcast.172, f32[512]{0:T(512)S(1)} %bitcast.176, ...), kind=kOutput, calls=%fused_computation.29.clone.1 | convolution fusion | flops 1275068416 | bytes 940036 | tf_op jit(solution)/shard_map/while/body/eval_jaxpr/dot_general | solution.py:124
  1010.7 50.4 %fusion.131 = f32[16,24,512]{2,1,0:T(8,128)S(1)} fusion(f32[16,24,512]{2,1,0:T(8,128)S(1)} %get-tuple-element.265, s32[]{:T(128)S(6)} %copy.108, f32[24,8192]{1,0:T(8,128)S(1)} %get-tuple-element.277, f32[8192]{0:T(1024)S(1)} %bitcast.171, f32[512]{0:T(512)S(1)} %bitcast.177, f32[8192]{0:T(1024)S(1)} %bitcast.172, f32[512]{0:T(512)S(1)} %bitcast.176, ...), kind=kOutput, calls=%fused_computation.29.clone.1 | convolution fusion | flops 1275068416 | bytes 940036 | tf_op jit(solution)/shard_map/while/body/eval_jaxpr/dot_general | solution.py:124
  1061.2 50.4 %fusion.131 = f32[16,24,512]{2,1,0:T(8,128)S(1)} fusion(f32[16,24,512]{2,1,0:T(8,128)S(1)} %get-tuple-element.265, s32[]{:T(128)S(6)} %copy.108, f32[24,8192]{1,0:T(8,128)S(1)} %get-tuple-element.277, f32[8192]{0:T(1024)S(1)} %bitcast.171, f32[512]{0:T(512)S(1)} %bitcast.177, f32[8192]{0:T(1024)S(1)} %bitcast.172, f32[512]{0:T(512)S(1)} %bitcast.176, ...), kind=kOutput, calls=%fused_computation.29.clone.1 | convolution fusion | flops 1275068416 | bytes 940036 | tf_op jit(solution)/shard_map/while/body/eval_jaxpr/dot_general | solution.py:124
  1111.8 50.4 %fusion.131 = f32[16,24,512]{2,1,0:T(8,128)S(1)} fusion(f32[16,24,512]{2,1,0:T(8,128)S(1)} %get-tuple-element.265, s32[]{:T(128)S(6)} %copy.108, f32[24,8192]{1,0:T(8,128)S(1)} %get-tuple-element.277, f32[8192]{0:T(1024)S(1)} %bitcast.171, f32[512]{0:T(512)S(1)} %bitcast.177, f32[8192]{0:T(1024)S(1)} %bitcast.172, f32[512]{0:T(512)S(1)} %bitcast.176, ...), kind=kOutput, calls=%fused_computation.29.clone.1 | convolution fusion | flops 1275068416 | bytes 940036 | tf_op jit(solution)/shard_map/while/body/eval_jaxpr/dot_general | solution.py:124
  1162.3 50.4 %fusion.131 = f32[16,24,512]{2,1,0:T(8,128)S(1)} fusion(f32[16,24,512]{2,1,0:T(8,128)S(1)} %get-tuple-element.265, s32[]{:T(128)S(6)} %copy.108, f32[24,8192]{1,0:T(8,128)S(1)} %get-tuple-element.277, f32[8192]{0:T(1024)S(1)} %bitcast.171, f32[512]{0:T(512)S(1)} %bitcast.177, f32[8192]{0:T(1024)S(1)} %bitcast.172, f32[512]{0:T(512)S(1)} %bitcast.176, ...), kind=kOutput, calls=%fused_computation.29.clone.1 | convolution fusion | flops 1275068416 | bytes 940036 | tf_op jit(solution)/shard_map/while/body/eval_jaxpr/dot_general | solution.py:124
  (149 shorter events, 234.0 us)
Async XLA Ops:
  0.6 6.3 copy-start.1
  5.8 8.1 copy-start
  6.7 7.1 copy-start.3
  6.8 207.0 %collective-permute-start = (f32[24,256]{1,0:T(8,128)S(1)}, f32[24,256]{1,0:T(8,128)}, u32[]{:S(2)}, u32[]{:S(2)}) collective-permute-start(f32[24,256]{1,0:T(8,128)S(1)} %fusion.63), channel_id=1, source_target_pairs={{0,8},{8,0},{16,24},{24,16},{1,9},{9,1},{17,25},{25,17},{2,10},{10... | collective-permute-start | bytes 73736 | tf_op jit(solution)/shard_map/ppermute | solution.py:107
  185.5 91.2 %copy-start.2 = (f32[1,1,256,1,512]{4,3,2,1,0:T(1,128)S(1)}, f32[1,1,256,1,512]{4,3,2,1,0:T(1,128)}, u32[]{:S(2)}) copy-start(f32[1,1,256,1,512]{4,3,2,1,0:T(1,128)} %get-tuple-element.193) | copy-start | bytes 1572868
  214.5 18.5 %collective-permute-start.1 = (f32[24,256]{1,0:T(8,128)S(1)}, f32[24,256]{1,0:T(8,128)S(1)}, u32[]{:S(2)}, u32[]{:S(2)}) collective-permute-start(f32[24,256]{1,0:T(8,128)S(1)} %add.116), channel_id=1, source_target_pairs={{0,16},{8,24},{16,0},{24,8},{1,17},{9,25},{17,1},{25,9},{2,18},{10... | collective-permute-start | bytes 73736 | tf_op jit(solution)/shard_map/ppermute | solution.py:107
  265.1 9.0 collective-permute-start.2
  274.0 2.7 collective-permute-start.3
  306.2 52.7 %copy-start.6 = (f32[3,4,16,128]{3,2,1,0:T(8,128)S(1)}, f32[3,4,16,128]{3,2,1,0:T(8,128)}, u32[]{:S(2)}) copy-start(f32[3,4,16,128]{3,2,1,0:T(8,128)} %param.27) | copy-start | bytes 294916
  306.2 9.2 collective-permute-start.4
  315.4 2.7 collective-permute-start.5
  349.5 55.0 %copy-start.4 = (f32[3,8192]{1,0:T(4,128)S(1)}, f32[3,8192]{1,0:T(4,128)}, u32[]{:S(2)}) copy-start(f32[3,8192]{1,0:T(4,128)} %param.26) | copy-start | bytes 294916
  349.5 9.2 collective-permute-start.6
  358.8 2.7 collective-permute-start.7
  361.8 42.7 %copy-start.8 = (f32[16,24,512]{2,1,0:T(8,128)S(1)}, f32[16,24,512]{2,1,0:T(8,128)}, u32[]{:S(2)}) copy-start(f32[16,24,512]{2,1,0:T(8,128)} %custom-call.1) | copy-start | bytes 2359300
  1213.3 6.1 copy-start.7
  1213.4 11.2 copy-start.5
  1213.4 5.9 collective-permute-start.8
  1216.8 7.0 collective-permute-start.9
  1224.6 8.5 collective-permute-start.11
  1225.9 7.2 collective-permute-start.10
